TPU v7x, 32 devices: a whole 2x2x4 slice. The times are simulated.
32 devices in a mesh: lon: 16 (over z, x, core), lat: 2 (over y).
Axes of the slice: x: 2, y: 2, z: 4, core: 2. Of those that a mesh axis runs over, the one named last changes fastest.
Arguments:
- state: float32 [5, 1, 5760, 256], P(None, None, 'lon', 'lat'), may hold values from -3 to 3
- cutoffs: int32 [2, 128], replicated, may hold values from 1 to 2879, as said below
Outputs:
- advanced: float32 [5, 1, 5760, 256], P(None, None, 'lon', 'lat')
Inputs may be any that keep to these rules, and one draw needn't show every extreme that they name: cutoffs[0, j] is the highest zonal wavenumber kept in row j and cutoffs[1, j] that of row 255 - j; in both caps the row at the pole keeps 1 and row 127 from the pole keeps 2880 - 1.
All inputs are finite; a program needn't handle non-finite values.
Results may differ from a plain program's by a relative error of at most 0.0003.
Values sent between devices are 32-bit elements; how exact they have to be, the bound alone decides.
A program may use at most 64 MiB of HBM per device.

v0:
```python
import jax
import jax.numpy as jnp
from jax import lax
from jax.sharding import PartitionSpec as P

SUBSTEPS = 2


time_step = 0.5
gravity_scale = 0.25
coriolis_scale = 0.5
wind_sign = (1.0, -1.0, -1.0, 1.0, 1.0)
highest = lax.Precision.HIGHEST
inner_factor = 64


def passed_along(value, axis, steps):
    count = lax.axis_size(axis)
    pairs = [(source, (source + steps) % count) for source in range(count)]
    return lax.ppermute(value, axis, pairs)


def extended(array, sides, width, wrap):
    for axis, dim in sides:
        peers, length = (lax.axis_size(axis), array.shape[dim])
        up = [(i, (i + 1) % peers) for i in range(peers if wrap else peers - 1)]
        down = [(j, i) for i, j in up]
        last = lax.slice_in_dim(array, length - width, length, axis=dim)
        initial = lax.slice_in_dim(array, 0, width, axis=dim)
        before = lax.ppermute(last, axis, up)
        after = lax.ppermute(initial, axis, down)
        array = jnp.concatenate([before, array, after], axis=dim)
    return array


def interface_flux(halo_padded, transported_field, advection_axis, extent_length):

    def shifted(offset):
        return lax.slice_in_dim(
            halo_padded, offset, offset + extent_length + 1, axis=advection_axis
        )

    far_west, mid_west, near_west, centre, near_east, far_east = [
        shifted(offset) for offset in range(6)
    ]
    interface_velocity = 0.5 * (
        lax.slice_in_dim(transported_field, 2, extent_length + 3, axis=advection_axis)
        + lax.slice_in_dim(transported_field, 3, extent_length + 4, axis=advection_axis)
    )
    central = (
        37.0 * (centre + near_west) - 8.0 * (near_east + mid_west) + (far_east + far_west)
    ) / 60.0
    upwind = (
        far_east - far_west - 5.0 * (near_east - mid_west) + 10.0 * (centre - near_west)
    ) / 60.0
    return interface_velocity * central - jnp.abs(interface_velocity) * upwind


def latitude_rows(first_row, row_count, total_rows):
    centres = (first_row + jnp.arange(row_count, dtype=jnp.int32)).astype(jnp.float32) + 0.5
    centre_cos = jnp.sin(centres * (jnp.pi / total_rows))
    centre_sin = -jnp.cos(centres * (jnp.pi / total_rows))
    faces = first_row + jnp.arange(row_count + 1, dtype=jnp.int32)
    face_cos = jnp.sin(
        jnp.minimum(faces, total_rows - faces).astype(jnp.float32) * (jnp.pi / total_rows)
    )
    return (centre_cos, centre_sin, face_cos)


def geopotential(fields):
    layer_mass = fields[0] * fields[3]
    return gravity_scale * jnp.flip(jnp.cumsum(jnp.flip(layer_mass, 0), axis=0), 0)


def zonal_tendency(lon_padded, centre_cos):
    lon_cells = lon_padded.shape[2] - 6
    face_fluxes = interface_flux(lon_padded, lon_padded[1:2], 2, lon_cells)
    zonal = face_fluxes[:, :, :-1] - face_fluxes[:, :, 1:]
    height = geopotential(lon_padded)
    height_slope = 0.5 * (height[:, 4 : lon_cells + 4] - height[:, 2 : lon_cells + 2])
    zonal = jnp.concatenate([zonal[:1], zonal[1:2] - height_slope[None], zonal[2:]], axis=0)
    return zonal / centre_cos


def phase_table(first, second, modulus, total):
    angle = (first[:, None] * second[None, :] % modulus).astype(jnp.float32) * (
        2.0 * jnp.pi / total
    )
    return (jnp.cos(angle), jnp.sin(angle))


def truncate_rows(rows, row_limit, lon_total):
    row_count = rows.shape[0]
    outer = lon_total // inner_factor
    outer_index = jnp.arange(outer, dtype=jnp.int32)
    inner_index = jnp.arange(inner_factor, dtype=jnp.int32)
    outer_cos, outer_sin = phase_table(outer_index, outer_index, outer, outer)
    twist_cos, twist_sin = phase_table(outer_index, inner_index, lon_total, lon_total)
    inner_cos, inner_sin = phase_table(inner_index, inner_index, inner_factor, inner_factor)
    folded = rows.reshape(row_count, outer, inner_factor)
    first_re = jnp.einsum("rpq,pk->rkq", folded, outer_cos, precision=highest)
    first_im = -jnp.einsum("rpq,pk->rkq", folded, outer_sin, precision=highest)
    turned_re = first_re * twist_cos + first_im * twist_sin
    turned_im = first_im * twist_cos - first_re * twist_sin
    spec_re = jnp.einsum("rkq,qj->rkj", turned_re, inner_cos, precision=highest) + jnp.einsum(
        "rkq,qj->rkj", turned_im, inner_sin, precision=highest
    )
    spec_im = jnp.einsum("rkq,qj->rkj", turned_im, inner_cos, precision=highest) - jnp.einsum(
        "rkq,qj->rkj", turned_re, inner_sin, precision=highest
    )
    wave = outer_index[:, None] + outer * inner_index[None, :]
    wave = jnp.minimum(wave, lon_total - wave).astype(jnp.float32)
    kept = wave[None, :, :] <= row_limit[:, None, None]
    spec_re = jnp.where(kept, spec_re, 0.0)
    spec_im = jnp.where(kept, spec_im, 0.0)
    back_re = jnp.einsum("rkj,qj->rkq", spec_re, inner_cos, precision=highest) - jnp.einsum(
        "rkj,qj->rkq", spec_im, inner_sin, precision=highest
    )
    back_im = jnp.einsum("rkj,qj->rkq", spec_re, inner_sin, precision=highest) + jnp.einsum(
        "rkj,qj->rkq", spec_im, inner_cos, precision=highest
    )
    untwist_re = back_re * twist_cos - back_im * twist_sin
    untwist_im = back_re * twist_sin + back_im * twist_cos
    result = jnp.einsum("rkq,pk->rpq", untwist_re, outer_cos, precision=highest) - jnp.einsum(
        "rkq,pk->rpq", untwist_im, outer_sin, precision=highest
    )
    return result.reshape(row_count, lon_total) / lon_total


def crossing_rims(state, is_south, is_north):
    lat_cells = state.shape[3]
    lon_count = lax.axis_size("lon")
    wind_flip = jnp.array(wind_sign, dtype=jnp.float32)[:, None, None, None]
    pole_rows = jnp.where(is_south, state[..., 0:2], state[..., lat_cells - 2 :])
    partner = passed_along(pole_rows, "lon", lon_count // 2) * wind_flip
    lat_halo = extended(state, (("lat", 3),), 3, False)
    south_rim = jnp.where(
        is_south,
        jnp.concatenate([lat_halo[..., 0:1], partner[..., 1:2], partner[..., 0:1]], axis=3),
        lat_halo[..., 0:3],
    )
    north_rim = jnp.where(
        is_north,
        jnp.concatenate(
            [partner[..., 1:2], partner[..., 0:1], lat_halo[..., lat_cells + 5 :]], axis=3
        ),
        lat_halo[..., lat_cells + 3 :],
    )
    return jnp.concatenate([south_rim, state, north_rim], axis=3)


def advance(state, geometry, cutoff_row, is_south, is_north):
    centre_cos, centre_sin, face_cos = geometry
    field_count, level_count, lon_cells, lat_cells = state.shape
    lon_count = lax.axis_size("lon")
    lon_total = lon_cells * lon_count
    lon_padded = extended(state, (("lon", 2),), 3, True)
    zonal = zonal_tendency(lon_padded, centre_cos)
    row_block = jnp.transpose(zonal, (0, 1, 3, 2)).reshape(lon_count, -1, lon_cells)
    row_limits = jnp.broadcast_to(cutoff_row, (field_count, level_count, lat_cells)).reshape(
        lon_count, -1, 1
    )
    values = lax.all_to_all(row_block, "lon", split_axis=0, concat_axis=2, tiled=True)
    limits = lax.all_to_all(row_limits, "lon", split_axis=0, concat_axis=2, tiled=True)
    spread = truncate_rows(values[0], limits[0, :, 0], lon_total)[None]
    returned = lax.all_to_all(spread, "lon", split_axis=2, concat_axis=0, tiled=True)
    filtered = jnp.transpose(
        returned.reshape(field_count, level_count, lat_cells, lon_cells), (0, 1, 3, 2)
    )
    zonal = jnp.where(jnp.logical_or(is_south, is_north), filtered, zonal)
    lat_padded = crossing_rims(state, is_south, is_north)
    merid_fluxes = interface_flux(lat_padded, lat_padded[2:3], 3, lat_cells) * face_cos
    meridional = (merid_fluxes[..., :-1] - merid_fluxes[..., 1:]) / centre_cos
    height = geopotential(lat_padded)
    north_slope = 0.5 * (height[..., 4 : lat_cells + 4] - height[..., 2 : lat_cells + 2])
    turning = coriolis_scale * centre_sin
    flux_tendency = zonal + meridional
    east_wind = flux_tendency[1] + turning * state[2]
    north_wind = flux_tendency[2] - turning * state[1] - north_slope
    flux_tendency = jnp.concatenate(
        [flux_tendency[:1], east_wind[None], north_wind[None], flux_tendency[3:]], axis=0
    )
    return state + time_step * flux_tendency


def shards(state, cutoffs):
    lat_index = lax.axis_index("lat")
    lat_count = lax.axis_size("lat")
    lat_cells = state.shape[3]
    geometry = latitude_rows(lat_index * lat_cells, lat_cells, lat_cells * lat_count)
    is_south = lat_index == 0
    is_north = lat_index == lat_count - 1
    north_row = jnp.where(is_north, jnp.flip(cutoffs[1], 0), -1)
    cutoff_row = jnp.where(is_south, cutoffs[0], north_row).astype(jnp.float32)
    for substep_index in range(SUBSTEPS):
        state = advance(state, geometry, cutoff_row, is_south, is_north)
    return state


def solution(mesh):
    return jax.shard_map(
        shards,
        mesh=mesh,
        in_specs=(P(None, None, "lon", "lat"), P()),
        out_specs=P(None, None, "lon", "lat"),
        check_vma=False,
    )
```

profile of v0, /device:TPU:9, one launch (start us, length us, event | category | flops | bytes accessed | tf_op | source)
XLA Modules:
  0.0 308.5 jit_solution(16900312575509501687)
XLA Ops:
  4.8 8.6 %all-to-all-start = ((f32[16,40,1]{1,2,0:T(1,128)}), f32[16,40,1]{1,2,0:T(1,128)S(1)}, u32[]{:S(2)}, u32[]{:S(2)}) async-start(f32[16,40,1]{1,2,0:T(1,128)} %bitcast.2), calls=%async_computation | async-start | bytes 16384 | tf_op jit(solution)/shard_map/all_to_all | solution.py:164
  18.1 5.3 %all-to-all-start.1 = ((f32[16,40,360]{2,1,0:T(8,128)}), f32[16,40,360]{2,1,0:T(8,128)S(1)}, u32[]{:S(2)}, u32[]{:S(2)}) async-start(f32[16,40,360]{2,1,0:T(8,128)} %bitcast.260), calls=%async_computation.1 | async-start | bytes 1966080 | tf_op jit(solution)/shard_map/all_to_all | solution.py:163
  34.0 4.0 %collective-permute-start.4 = (f32[5,1,360,3]{2,1,3,0:T(1,128)S(1)}, f32[5,1,360,3]{2,1,3,0:T(1,128)S(1)}, u32[]{:S(2)}, u32[]{:S(2)}) collective-permute-start(f32[5,1,360,3]{2,1,3,0:T(1,128)S(1)} %copy.270), channel_id=1, source_target_pairs={{0,1},{2,3},{4,5},{6,7},{8,9},{10,11},{12,13},{14,15},{16,17},{18,... | collective-permute-start | bytes 64808 | tf_op jit(solution)/shard_map/ppermute | solution.py:30
  38.4 8.9 %all-to-all-done.1 = f32[16,40,360]{2,1,0:T(8,128)S(1)} async-done(((f32[16,40,360]{2,1,0:T(8,128)}), f32[16,40,360]{2,1,0:T(8,128)S(1)}, u32[]{:S(2)}, u32[]{:S(2)}) %all-to-all-start.1) | async-done | bytes 921632 | tf_op jit(solution)/shard_map/all_to_all | solution.py:163
  73.1 3.6 %copy.259 = f32[40,90,64]{0,2,1:T(8,128)} copy(f32[40,90,64]{1,2,0:T(8,128)S(1)} %multiply_bitcast_fusion.1) | data formatting | bytes 1843200 | tf_op jit(solution)/shard_map/div | solution.py:127
  77.3 27.7 %reduce = f32[5760,40]{1,0:T(8,128)} reduce(f32[5760,1,40]{2,1,0:T(1,128)} %bitcast.246, f32[]{:T(128)} %broadcast.641), dimensions={1}, to_apply=%bitcast.202.reduce_sub_computation | reduce | bytes 1843204
  105.0 4.8 %reshape.638 = f32[16,1,14400]{2,1,0:T(1,128)} reshape(f32[5760,40]{1,0:T(8,128)} %reduce) | data formatting | bytes 1843200
  109.8 5.3 %all-to-all-start.2 = ((f32[16,1,14400]{2,1,0:T(1,128)}), f32[16,1,14400]{2,1,0:T(1,128)}, u32[]{:S(2)}, u32[]{:S(2)}) async-start(f32[16,1,14400]{2,1,0:T(1,128)} %reshape.638), calls=%async_computation.2 | async-start | bytes 1851392 | tf_op jit(solution)/shard_map/all_to_all | solution.py:166
  125.2 3.6 %subtract_multiply_fusion.1 = f32[5,1,360,129]{3,2,1,0:T(8,128)S(1)} fusion(f32[5,1,360,3]{3,2,1,0:T(8,128)S(1)} %get-tuple-element.20, f32[5,1,360,128]{3,2,1,0:T(8,128)S(1)} %copy-done, f32[5,1,360,3]{3,2,1,0:T(8,128)S(1)} %get-tuple-element.19, f32[129]{0:T(256)S(1)} %fusion.173, f32[360,129]{1,0:T(8,128)S(1)} %multiply_bitcast_fusion.4, ...), kind=kLoop, calls=%fused_computation.41 | loop fusion | flops 5572800 | bytes 2265636 | tf_op jit(solution)/shard_map/mul | solution.py:172
  128.8 8.7 %all-to-all-done.2 = f32[16,1,14400]{2,1,0:T(1,128)} async-done(((f32[16,1,14400]{2,1,0:T(1,128)}), f32[16,1,14400]{2,1,0:T(1,128)}, u32[]{:S(2)}, u32[]{:S(2)}) %all-to-all-start.2) | async-done | bytes 921632 | tf_op jit(solution)/shard_map/all_to_all | solution.py:166
  137.5 4.9 %reduce.1 = f32[16,14400]{1,0:T(8,128)} reduce(f32[16,1,14400]{2,1,0:T(1,128)} %all-to-all-done.2, f32[]{:T(128)} %broadcast.641), dimensions={1}, to_apply=%all_to_all.69.reduce_sub_computation | reduce | bytes 1843204 | tf_op jit(solution)/shard_map/all_to_all | solution.py:166
  142.4 8.8 %reshape.639 = f32[5760,1,40]{2,1,0:T(1,128)} reshape(f32[16,14400]{1,0:T(8,128)} %reduce.1) | data formatting | bytes 1843200
  165.4 9.8 %all-to-all-start.3 = ((f32[16,40,360]{2,1,0:T(8,128)}), f32[16,40,360]{2,1,0:T(8,128)S(1)}, u32[]{:S(2)}, u32[]{:S(2)}) async-start(f32[16,40,360]{2,1,0:T(8,128)} %bitcast.261), calls=%async_computation.3 | async-start | bytes 1966080 | tf_op jit(solution)/shard_map/all_to_all | solution.py:163
  181.0 4.0 %collective-permute-start.9 = (f32[5,1,360,3]{2,1,3,0:T(1,128)S(1)}, f32[5,1,360,3]{2,1,3,0:T(1,128)S(1)}, u32[]{:S(2)}, u32[]{:S(2)}) collective-permute-start(f32[5,1,360,3]{2,1,3,0:T(1,128)S(1)} %copy.244), channel_id=1, source_target_pairs={{0,1},{2,3},{4,5},{6,7},{8,9},{10,11},{12,13},{14,15},{16,17},{18,... | collective-permute-start | bytes 64808 | tf_op jit(solution)/shard_map/ppermute | solution.py:30
  190.0 9.3 %all-to-all-done.3 = f32[16,40,360]{2,1,0:T(8,128)S(1)} async-done(((f32[16,40,360]{2,1,0:T(8,128)}), f32[16,40,360]{2,1,0:T(8,128)S(1)}, u32[]{:S(2)}, u32[]{:S(2)}) %all-to-all-start.3) | async-done | bytes 921632 | tf_op jit(solution)/shard_map/all_to_all | solution.py:163
  224.6 3.6 %copy.264 = f32[40,90,64]{0,2,1:T(8,128)} copy(f32[40,90,64]{1,2,0:T(8,128)S(1)} %multiply_bitcast_fusion) | data formatting | bytes 1843200 | tf_op jit(solution)/shard_map/div | solution.py:127
  228.2 27.7 %reduce.2 = f32[5760,40]{1,0:T(8,128)} reduce(f32[5760,1,40]{2,1,0:T(1,128)} %bitcast.248, f32[]{:T(128)} %broadcast.641), dimensions={1}, to_apply=%bitcast.204.reduce_sub_computation | reduce | bytes 1843204
  255.9 4.8 %reshape.640 = f32[16,1,14400]{2,1,0:T(1,128)} reshape(f32[5760,40]{1,0:T(8,128)} %reduce.2) | data formatting | bytes 1843200
  260.7 5.1 %all-to-all-start.4 = ((f32[16,1,14400]{2,1,0:T(1,128)}), f32[16,1,14400]{2,1,0:T(1,128)S(1)}, u32[]{:S(2)}, u32[]{:S(2)}) async-start(f32[16,1,14400]{2,1,0:T(1,128)} %reshape.640), calls=%async_computation.4 | async-start | bytes 1851392 | tf_op jit(solution)/shard_map/all_to_all | solution.py:166
  273.6 3.9 %maximum_select_fusion.3 = (f32[5,1,360,3]{3,2,1,0:T(8,128)S(1)}, f32[5,1,360,3]{3,2,1,0:T(8,128)S(1)}) fusion(f32[5,1,360,3]{3,2,1,0:T(8,128)} %copy.246, f32[5,1,360,1]{3,2,1,0:T(8,128)} %copy.272, f32[5,1,360,1]{3,2,1,0:T(8,128)} %copy.271, f32[5,1,360,1]{3,2,1,0:T(8,128)} %copy.245, pred[]{:T(512)S(6)} %eq.15, f32[5,1,360,3]{3,2,1,0:T(8,128)} %copy.243, ...), kind=kLoop, calls=%fused_computation.108 | loop fusion | flops 32400 | bytes 115202 | tf_op jit(solution)/shard_map/jit(_where)/select_n | solution.py:137
  278.1 4.5 %subtract_multiply_fusion = f32[5,1,360,129]{3,2,1,0:T(8,128)} fusion(f32[5,1,360,3]{3,2,1,0:T(8,128)S(1)} %get-tuple-element.18, f32[5,1,360,128]{3,2,1,0:T(8,128)S(1)} %fusion.37, f32[5,1,360,3]{3,2,1,0:T(8,128)S(1)} %get-tuple-element.17, f32[360,129]{1,0:T(8,128)S(1)} %multiply_bitcast_fusion.2, f32[360,129]{1,0:T(8,128)S(1)} %get-tuple-element.7, ...), kind=kLoop, calls=%fused_computation.40 | loop fusion | flops 5572800 | bytes 2265636 | tf_op jit(solution)/shard_map/mul | solution.py:172
  282.7 5.5 %all-to-all-done.4 = f32[16,1,14400]{2,1,0:T(1,128)S(1)} async-done(((f32[16,1,14400]{2,1,0:T(1,128)}), f32[16,1,14400]{2,1,0:T(1,128)S(1)}, u32[]{:S(2)}, u32[]{:S(2)}) %all-to-all-start.4) | async-done | bytes 921632 | tf_op jit(solution)/shard_map/all_to_all | solution.py:166
  288.2 4.1 %reduce.3 = f32[16,14400]{1,0:T(8,128)} reduce(f32[16,1,14400]{2,1,0:T(1,128)S(1)} %all-to-all-done.4, f32[]{:T(128)} %broadcast.641), dimensions={1}, to_apply=%all_to_all.75.reduce_sub_computation | reduce | bytes 1843204 | tf_op jit(solution)/shard_map/all_to_all | solution.py:166
  292.2 8.8 %reshape.641 = f32[5760,1,40]{2,1,0:T(1,128)} reshape(f32[16,14400]{1,0:T(8,128)} %reduce.3) | data formatting | bytes 1843200
  (146 shorter events, 122.5 us)
Async XLA Ops:
  0.0 14.7 %copy-start = (f32[5,1,360,128]{3,2,1,0:T(8,128)S(1)}, f32[5,1,360,128]{3,2,1,0:T(8,128)}, u32[]{:S(2)}) copy-start(f32[5,1,360,128]{3,2,1,0:T(8,128)} %param.4) | copy-start | bytes 2764804
  0.8 13.9 %collective-permute-start = (f32[5,1,3,128]{3,2,1,0:T(4,128)S(1)}, f32[5,1,3,128]{3,2,1,0:T(4,128)S(1)}, u32[]{:S(2)}, u32[]{:S(2)}) collective-permute-start(f32[5,1,3,128]{3,2,1,0:T(4,128)S(1)} %get-tuple-element.33), channel_id=1, source_target_pairs={{2,0},{4,2},{6,4},{8,6},{10,8},{12,10},{14,12},{16,14},{18,16},{20... | collective-permute-start | bytes 23048 | tf_op jit(solution)/shard_map/ppermute | solution.py:31
  1.5 13.2 %collective-permute-start.1 = (f32[5,1,3,128]{3,2,1,0:T(4,128)S(1)}, f32[5,1,3,128]{3,2,1,0:T(4,128)S(1)}, u32[]{:S(2)}, u32[]{:S(2)}) collective-permute-start(f32[5,1,3,128]{3,2,1,0:T(4,128)S(1)} %get-tuple-element.34), channel_id=1, source_target_pairs={{0,2},{2,4},{4,6},{6,8},{8,10},{10,12},{12,14},{14,16},{16,18},{18... | collective-permute-start | bytes 23048 | tf_op jit(solution)/shard_map/ppermute | solution.py:30
  4.8 13.3 %all-to-all-start = ((f32[16,40,1]{1,2,0:T(1,128)}), f32[16,40,1]{1,2,0:T(1,128)S(1)}, u32[]{:S(2)}, u32[]{:S(2)}) async-start(f32[16,40,1]{1,2,0:T(1,128)} %bitcast.2), calls=%async_computation | async-start | bytes 16384 | tf_op jit(solution)/shard_map/all_to_all | solution.py:164
  15.9 1.4 copy-start.1
  15.9 1.4 copy-start.2
  18.1 29.2 %all-to-all-start.1 = ((f32[16,40,360]{2,1,0:T(8,128)}), f32[16,40,360]{2,1,0:T(8,128)S(1)}, u32[]{:S(2)}, u32[]{:S(2)}) async-start(f32[16,40,360]{2,1,0:T(8,128)} %bitcast.260), calls=%async_computation.1 | async-start | bytes 1966080 | tf_op jit(solution)/shard_map/all_to_all | solution.py:163
  26.1 89.0 %collective-permute-start.2 = (f32[5,1,360,2]{2,3,1,0:T(2,128)S(1)}, f32[5,1,360,2]{2,3,1,0:T(2,128)S(1)}, u32[]{:S(2)}, u32[]{:S(2)}) collective-permute-start(f32[5,1,360,2]{2,3,1,0:T(2,128)S(1)} %copy.215), channel_id=1, source_target_pairs={{0,16},{2,18},{4,20},{6,22},{8,24},{10,26},{12,28},{14,30},{16,0},... | collective-permute-start | bytes 43208 | tf_op jit(solution)/shard_map/ppermute | solution.py:20
  31.2 84.6 %collective-permute-start.3 = (f32[5,1,360,3]{2,1,3,0:T(1,128)S(1)}, f32[5,1,360,3]{2,1,3,0:T(1,128)S(1)}, u32[]{:S(2)}, u32[]{:S(2)}) collective-permute-start(f32[5,1,360,3]{2,1,3,0:T(1,128)S(1)} %copy.269), channel_id=1, source_target_pairs={{1,0},{3,2},{5,4},{7,6},{9,8},{11,10},{13,12},{15,14},{17,16},{19,... | collective-permute-start | bytes 64808 | tf_op jit(solution)/shard_map/ppermute | solution.py:31
  34.0 83.1 %collective-permute-start.4 = (f32[5,1,360,3]{2,1,3,0:T(1,128)S(1)}, f32[5,1,360,3]{2,1,3,0:T(1,128)S(1)}, u32[]{:S(2)}, u32[]{:S(2)}) collective-permute-start(f32[5,1,360,3]{2,1,3,0:T(1,128)S(1)} %copy.270), channel_id=1, source_target_pairs={{0,1},{2,3},{4,5},{6,7},{8,9},{10,11},{12,13},{14,15},{16,17},{18,... | collective-permute-start | bytes 64808 | tf_op jit(solution)/shard_map/ppermute | solution.py:30
  109.8 5.3 %copy-start.4 = (f32[5]{0:T(128)S(1)}, f32[5]{0:T(128)}, u32[]{:S(2)}) copy-start(f32[5]{0:T(128)} %constant.123.clone) | copy-start | bytes 64
  109.8 27.7 %all-to-all-start.2 = ((f32[16,1,14400]{2,1,0:T(1,128)}), f32[16,1,14400]{2,1,0:T(1,128)}, u32[]{:S(2)}, u32[]{:S(2)}) async-start(f32[16,1,14400]{2,1,0:T(1,128)} %reshape.638), calls=%async_computation.2 | async-start | bytes 1851392 | tf_op jit(solution)/shard_map/all_to_all | solution.py:166
  158.4 1.0 copy-start.3
  159.7 3.2 %collective-permute-start.5 = (f32[5,1,3,128]{3,2,1,0:T(4,128)S(1)}, f32[5,1,3,128]{3,2,1,0:T(4,128)S(1)}, u32[]{:S(2)}, u32[]{:S(2)}) collective-permute-start(f32[5,1,3,128]{3,2,1,0:T(4,128)S(1)} %get-tuple-element.26), channel_id=1, source_target_pairs={{2,0},{4,2},{6,4},{8,6},{10,8},{12,10},{14,12},{16,14},{18,16},{20... | collective-permute-start | bytes 23048 | tf_op jit(solution)/shard_map/ppermute | solution.py:31
  159.8 3.1 %collective-permute-start.6 = (f32[5,1,3,128]{3,2,1,0:T(4,128)S(1)}, f32[5,1,3,128]{3,2,1,0:T(4,128)S(1)}, u32[]{:S(2)}, u32[]{:S(2)}) collective-permute-start(f32[5,1,3,128]{3,2,1,0:T(4,128)S(1)} %get-tuple-element.25), channel_id=1, source_target_pairs={{0,2},{2,4},{4,6},{6,8},{8,10},{10,12},{12,14},{14,16},{16,18},{18... | collective-permute-start | bytes 23048 | tf_op jit(solution)/shard_map/ppermute | solution.py:30
  165.4 33.8 %all-to-all-start.3 = ((f32[16,40,360]{2,1,0:T(8,128)}), f32[16,40,360]{2,1,0:T(8,128)S(1)}, u32[]{:S(2)}, u32[]{:S(2)}) async-start(f32[16,40,360]{2,1,0:T(8,128)} %bitcast.261), calls=%async_computation.3 | async-start | bytes 1966080 | tf_op jit(solution)/shard_map/all_to_all | solution.py:163
  178.2 90.2 %collective-permute-start.8 = (f32[5,1,360,3]{2,1,3,0:T(1,128)S(1)}, f32[5,1,360,3]{2,1,3,0:T(1,128)S(1)}, u32[]{:S(2)}, u32[]{:S(2)}) collective-permute-start(f32[5,1,360,3]{2,1,3,0:T(1,128)S(1)} %copy.241), channel_id=1, source_target_pairs={{1,0},{3,2},{5,4},{7,6},{9,8},{11,10},{13,12},{15,14},{17,16},{19,... | collective-permute-start | bytes 64808 | tf_op jit(solution)/shard_map/ppermute | solution.py:31
  181.0 88.7 %collective-permute-start.9 = (f32[5,1,360,3]{2,1,3,0:T(1,128)S(1)}, f32[5,1,360,3]{2,1,3,0:T(1,128)S(1)}, u32[]{:S(2)}, u32[]{:S(2)}) collective-permute-start(f32[5,1,360,3]{2,1,3,0:T(1,128)S(1)} %copy.244), channel_id=1, source_target_pairs={{0,1},{2,3},{4,5},{6,7},{8,9},{10,11},{12,13},{14,15},{16,17},{18,... | collective-permute-start | bytes 64808 | tf_op jit(solution)/shard_map/ppermute | solution.py:30
  187.8 78.0 %collective-permute-start.7 = (f32[5,1,360,2]{2,3,1,0:T(2,128)S(1)}, f32[5,1,360,2]{2,3,1,0:T(2,128)S(1)}, u32[]{:S(2)}, u32[]{:S(2)}) collective-permute-start(f32[5,1,360,2]{2,3,1,0:T(2,128)S(1)} %copy.237), channel_id=1, source_target_pairs={{0,16},{2,18},{4,20},{6,22},{8,24},{10,26},{12,28},{14,30},{16,0},... | collective-permute-start | bytes 43208 | tf_op jit(solution)/shard_map/ppermute | solution.py:20
  260.7 27.5 %all-to-all-start.4 = ((f32[16,1,14400]{2,1,0:T(1,128)}), f32[16,1,14400]{2,1,0:T(1,128)S(1)}, u32[]{:S(2)}, u32[]{:S(2)}) async-start(f32[16,1,14400]{2,1,0:T(1,128)} %reshape.640), calls=%async_computation.4 | async-start | bytes 1851392 | tf_op jit(solution)/shard_map/all_to_all | solution.py:166
where the time goes:
time: 314 us; the launch traced here: 308 us
  other arithmetic  93.3 us (30%)
  local copies, waits for them, and re-layouts  89.5 us (29%)
  starting transfers between devices  53 us (17%)
  matrix products  37.6 us (12%)
  waiting for transfers between devices  34.1 us (11%)
    unnamed x2, other arithmetic  55.4 us
    unnamed x22, local copies, waits for them, and re-layouts  36.1 us
    all_to_all x2, waiting for transfers between devices, advance(): lax.all_to_all(row_block, 'lon', split_axis=0, concat_axis=2, tiled=True)  18.2 us
    all_to_all x2, starting transfers between devices, advance(): lax.all_to_all(row_block, 'lon', split_axis=0, concat_axis=2, tiled=True)  15.1 us
    all_to_all x2, waiting for transfers between devices, advance(): lax.all_to_all(spread, 'lon', split_axis=2, concat_axis=0, tiled=True)  14.2 us
    unnamed x8, matrix products  11.3 us
    ppermute x4, starting transfers between devices, extended(): before = lax.ppermute(last, axis, up)  11.3 us
    another operation x4, local copies, waits for them, and re-layouts, truncate_rows(): folded = rows.reshape(row_count, outer, inner_factor)  10.7 us
  transfers between devices with their start and end apart: 15, of which 6 were waited for; matrix products, arithmetic and copies ran while one was open for 57% of the time, Pallas kernels for 0%

commit v1 on v0

--- a/solution.py
+++ b/solution.py
@@ -1,6 +1,11 @@
+import functools
+
 import jax
 import jax.numpy as jnp
+import numpy as np
 from jax import lax
+from jax.experimental import pallas as pl
+from jax.experimental.pallas import tpu as pltpu
 from jax.sharding import PartitionSpec as P
 
 SUBSTEPS = 2
@@ -12,6 +17,7 @@
 wind_sign = (1.0, -1.0, -1.0, 1.0, 1.0)
 highest = lax.Precision.HIGHEST
 inner_factor = 64
+MESH = pl.DeviceIdType.MESH
 
 
 def passed_along(value, axis, steps):
@@ -183,13 +189,502 @@
     return state + time_step * flux_tendency
 
 
+def circle_tables(count, width, lanes):
+    total = count * width
+    inner = np.arange(width)
+    angle = 2.0 * np.pi * (inner[:, None] * inner[None, :] % width) / width
+    table = np.zeros((lanes, 2 * lanes), np.float32)
+    table[:width, :width] = np.cos(angle)
+    table[:width, lanes : lanes + width] = np.sin(angle)
+    high = table.astype(jnp.bfloat16)
+    low = (table - high.astype(np.float32)).astype(jnp.bfloat16)
+    outer = np.arange(count // 2 + 1)
+    turn = 2.0 * np.pi * (outer[:, None] * np.arange(lanes)[None, :] % total) / total
+    twist = np.stack([np.cos(turn), np.sin(turn)]).astype(np.float32)
+    return high, low, twist
+
+
+def circle_kernel(
+    count, width, bands, x_ref, geo_ref, twist_ref, high_ref, low_ref, out_ref,
+    outgoing, states, incoming, filtered, carrier, spectrum, halo_out, halo_in,
+    first_send, first_recv, last_send, last_recv, halo_send, halo_recv,
+):
+    fields = x_ref.shape[0]
+    lanes = outgoing.shape[2]
+    rows = geo_ref.shape[1]
+    half = count // 2
+    total = count * width
+    me = lax.axis_index("lon")
+    lat = lax.axis_index("lat")
+    even = lax.rem(lat, 2) == 0
+
+    def band_of(device):
+        return jnp.where(even, device, count - 1 - device)
+
+    band = band_of(me)
+    at_south = jnp.logical_and(band == 0, lat == 0)
+    at_north = jnp.logical_and(band == count - 1, lat == bands - 1)
+    step = jnp.where(even, 1, -1)
+    south_lon = jnp.where(band == 0, me, me - step)
+    south_lat = jnp.where(band == 0, lat - 1, lat)
+    north_lon = jnp.where(band == count - 1, me, me + step)
+    north_lat = jnp.where(band == count - 1, lat + 1, lat)
+    lane = lax.broadcasted_iota(jnp.int32, (rows, lanes), 1)
+    inside = lane < width
+
+    barrier = pltpu.get_barrier_semaphore()
+
+    def greet(offset, carry):
+        peer = lax.rem(me + offset, count)
+        pl.semaphore_signal(barrier, inc=1, device_id={"lon": peer, "lat": lat}, device_id_type=MESH)
+        return carry
+
+    lax.fori_loop(1, count, greet, 0)
+    crosses_south = jnp.logical_and(band == 0, lat > 0)
+    crosses_north = jnp.logical_and(band == count - 1, lat < bands - 1)
+
+    @pl.when(crosses_south)
+    def _():
+        pl.semaphore_signal(barrier, inc=1, device_id={"lon": me, "lat": lat - 1}, device_id_type=MESH)
+
+    @pl.when(crosses_north)
+    def _():
+        pl.semaphore_signal(barrier, inc=1, device_id={"lon": me, "lat": lat + 1}, device_id_type=MESH)
+
+    def first_copy(field, peer, slot):
+        start = pl.multiple_of(band_of(peer) * rows, rows)
+        return pltpu.make_async_remote_copy(
+            src_ref=outgoing.at[field, pl.ds(start, rows), :],
+            dst_ref=states.at[0, field, slot, pl.ds(8, rows), :],
+            send_sem=first_send.at[field, peer],
+            recv_sem=first_recv.at[field, slot],
+            device_id={"lon": peer, "lat": lat},
+            device_id_type=MESH,
+        )
+
+    def last_copy(field, peer, owner):
+        start = pl.multiple_of(band_of(owner) * rows, rows)
+        return pltpu.make_async_remote_copy(
+            src_ref=states.at[2, field, peer, pl.ds(8, rows), :],
+            dst_ref=incoming.at[field, pl.ds(start, rows), :],
+            send_sem=last_send.at[field, peer],
+            recv_sem=last_recv.at[field, owner],
+            device_id={"lon": peer, "lat": lat},
+            device_id_type=MESH,
+        )
+
+    def over_peers(action):
+        def one(offset, carry):
+            action(lax.rem(me + offset, count))
+            return carry
+
+        lax.fori_loop(1, count, one, 0)
+
+    def halo_copy(turn, side, field):
+        return pltpu.make_async_remote_copy(
+            src_ref=halo_out.at[turn, side, field],
+            dst_ref=halo_in.at[turn, 1 - side, field],
+            send_sem=halo_send.at[turn, side, field],
+            recv_sem=halo_recv.at[turn, 1 - side, field],
+            device_id={
+                "lon": south_lon if side == 0 else north_lon,
+                "lat": south_lat if side == 0 else north_lat,
+            },
+            device_id_type=MESH,
+        )
+
+    def send_halo(turn, field):
+        for p in range(count):
+            halo_out[turn, 0, field, 3 * p : 3 * p + 3, :] = states[turn, field, p, 8:11, :]
+            halo_out[turn, 1, field, 3 * p : 3 * p + 3, :] = states[turn, field, p, rows + 5 : rows + 8, :]
+
+        @pl.when(jnp.logical_not(at_south))
+        def _():
+            halo_copy(turn, 0, field).start()
+
+        @pl.when(jnp.logical_not(at_north))
+        def _():
+            halo_copy(turn, 1, field).start()
+
+    def take_halo(turn, field):
+        sign = jnp.where(jnp.logical_or(field == 1, field == 2), -1.0, 1.0)
+
+        @pl.when(jnp.logical_not(at_south))
+        def _():
+            copy = halo_copy(turn, 0, field)
+            copy.wait_send()
+            arrival = pltpu.make_async_remote_copy(
+                src_ref=halo_out.at[turn, 0, field],
+                dst_ref=halo_in.at[turn, 0, field],
+                send_sem=halo_send.at[turn, 0, field],
+                recv_sem=halo_recv.at[turn, 0, field],
+                device_id={"lon": south_lon, "lat": south_lat},
+                device_id_type=MESH,
+            )
+            arrival.wait_recv()
+            for p in range(count):
+                states[turn, field, p, 5:8, :] = halo_in[turn, 0, field, 3 * p : 3 * p + 3, :]
+
+        @pl.when(at_south)
+        def _():
+            for p in range(count):
+                for m in range(3):
+                    states[turn, field, p, 7 - m : 8 - m, :] = (
+                        sign * states[turn, field, (p + half) % count, 8 + m : 9 + m, :]
+                    )
+
+        @pl.when(jnp.logical_not(at_north))
+        def _():
+            copy = halo_copy(turn, 1, field)
+            copy.wait_send()
+            arrival = pltpu.make_async_remote_copy(
+                src_ref=halo_out.at[turn, 1, field],
+                dst_ref=halo_in.at[turn, 1, field],
+                send_sem=halo_send.at[turn, 1, field],
+                recv_sem=halo_recv.at[turn, 1, field],
+                device_id={"lon": north_lon, "lat": north_lat},
+                device_id_type=MESH,
+            )
+            arrival.wait_recv()
+            for p in range(count):
+                states[turn, field, p, rows + 8 : rows + 11, :] = halo_in[
+                    turn, 1, field, 3 * p : 3 * p + 3, :
+                ]
+
+        @pl.when(at_north)
+        def _():
+            for p in range(count):
+                for m in range(3):
+                    states[turn, field, p, rows + 8 + m : rows + 9 + m, :] = (
+                        sign
+                        * states[turn, field, (p + half) % count, rows + 7 - m : rows + 8 - m, :]
+                    )
+
+    def arrive(field):
+        def one(peer):
+            first_copy(field, peer, peer).wait_recv()
+
+        over_peers(one)
+        send_halo(0, field)
+
+    def wrapped(turn, field, p):
+        east = lax.rem(p + 1, count)
+        west = lax.rem(p + count - 1, count)
+        core = states[turn, field, p, 8 : 8 + rows, :]
+        after = pltpu.roll(states[turn, field, east, 8 : 8 + rows, :], width, 1)
+        before = pltpu.roll(states[turn, field, west, 8 : 8 + rows, :], lanes - width, 1)
+        middle = width + (lanes - width) // 2
+        return jnp.where(inside, core, jnp.where(lane < middle, after, before))
+
+    def moved(value, offset):
+        return pltpu.roll(value, (-offset) % lanes, 1)
+
+    def face_flux(carrying, m3, m2, m1, c0, p1, p2):
+        central = 37.0 * (c0 + m1) - 8.0 * (p1 + m2) + (p2 + m3)
+        upwind = (p2 - m3) - 5.0 * (p1 - m2) + 10.0 * (c0 - m1)
+        return carrying * central - jnp.abs(carrying) * upwind
+
+    def over_tiles(action, group=2):
+        def one(block, carry):
+            for inner in range(group):
+                action(block * group + inner)
+            return carry
+
+        lax.fori_loop(0, count // group, one, 0)
+
+    chunks = [slice(128 * c, 128 * c + 128) for c in range(lanes // 128)]
+    waves = half + 1
+    block = waves * rows
+
+    def product():
+        value = spectrum[...]
+        high = value.astype(jnp.bfloat16)
+        low = (value - high.astype(jnp.float32)).astype(jnp.bfloat16)
+        weights = high_ref[...]
+        result = jnp.dot(high, weights, preferred_element_type=jnp.float32)
+        result += jnp.dot(low, weights, preferred_element_type=jnp.float32)
+        return result + jnp.dot(high, low_ref[...], preferred_element_type=jnp.float32)
+
+    def cos_of(k, p):
+        return float(np.cos(2.0 * np.pi * (k * p % count) / count))
+
+    def sin_of(k, p):
+        return float(np.sin(2.0 * np.pi * (k * p % count) / count))
+
+    def combined(terms):
+        value = None
+        for factor, term in terms:
+            if abs(factor) < 1e-9:
+                continue
+            if abs(abs(factor) - 1.0) < 1e-9:
+                scaled = term
+            else:
+                scaled = abs(factor) * term
+            if value is None:
+                value = scaled if factor > 0 else -scaled
+            elif factor > 0:
+                value = value + scaled
+            else:
+                value = value - scaled
+        return value
+
+    def truncate(field):
+        for cut in chunks:
+            z = [filtered[field, p, :, cut] for p in range(count)]
+            sums = [z[0]] + [z[p] + z[count - p] for p in range(1, half)] + [z[half]]
+            gaps = [None] + [z[p] - z[count - p] for p in range(1, half)]
+            for k in range(waves):
+                cosine = twist_ref[0, k : k + 1, cut]
+                sine = twist_ref[1, k : k + 1, cut]
+                real = combined([(cos_of(k, p), sums[p]) for p in range(half + 1)])
+                imag = combined([(-sin_of(k, p), gaps[p]) for p in range(1, half)])
+                if imag is None:
+                    turned_re, turned_im = real * cosine, -(real * sine)
+                else:
+                    turned_re = real * cosine + imag * sine
+                    turned_im = imag * cosine - real * sine
+                spectrum[k * rows : (k + 1) * rows, cut] = turned_re
+                spectrum[block + k * rows : block + (k + 1) * rows, cut] = turned_im
+        result = product()
+        limit = geo_ref[4]
+        for k in range(waves):
+            top = slice(k * rows, (k + 1) * rows)
+            low = slice(block + k * rows, block + (k + 1) * rows)
+            wave = k + count * lane
+            wave = jnp.minimum(wave, total - wave).astype(jnp.float32)
+            kept = wave <= limit
+            spectrum[top, :] = jnp.where(kept, result[top, :lanes] + result[low, lanes:], 0.0)
+            spectrum[low, :] = jnp.where(kept, result[low, :lanes] - result[top, lanes:], 0.0)
+        result = product()
+        scale = 1.0 / total
+        for c, cut in enumerate(chunks):
+            sin_cut = slice(lanes + 128 * c, lanes + 128 * c + 128)
+            reals, imags = [], []
+            for k in range(waves):
+                top = slice(k * rows, (k + 1) * rows)
+                low = slice(block + k * rows, block + (k + 1) * rows)
+                factor = scale if k in (0, half) else 2.0 * scale
+                cosine = twist_ref[0, k : k + 1, cut] * factor
+                sine = twist_ref[1, k : k + 1, cut] * factor
+                back_re = result[top, cut] - result[low, sin_cut]
+                back_im = result[top, sin_cut] + result[low, cut]
+                reals.append(back_re * cosine - back_im * sine)
+                imags.append(back_im * cosine + back_re * sine)
+            for p in range(half + 1):
+                even_part = combined([(cos_of(k, p), reals[k]) for k in range(waves)])
+                odd_part = combined([(sin_of(k, p), imags[k]) for k in range(1, half)])
+                if odd_part is None:
+                    filtered[field, p, :, cut] = even_part
+                else:
+                    filtered[field, p, :, cut] = even_part - odd_part
+                    filtered[field, count - p, :, cut] = even_part + odd_part
+
+    for index, field in enumerate((1, 0, 3, 4, 2)):
+        source = jnp.concatenate(
+            [x_ref[field], jnp.zeros((lanes - width, x_ref.shape[2]), jnp.float32)], axis=0
+        )
+        outgoing[field] = source.T
+        if index == 0:
+            expected = count - 1 + crosses_south.astype(jnp.int32) + crosses_north.astype(jnp.int32)
+            pl.semaphore_wait(barrier, expected)
+
+        def send(peer, field=field):
+            first_copy(field, peer, me).start()
+
+        over_peers(send)
+        own = pl.multiple_of(band * rows, rows)
+        states[0, field, me, 8 : 8 + rows, :] = outgoing[field, pl.ds(own, rows), :]
+
+    def substep(turn, carry):
+        @pl.when(turn == 0)
+        def _():
+            arrive(1)
+
+        def make_carrier(p):
+            wind = wrapped(turn, 1, p)
+            carrier[p] = (wind + moved(wind, -1)) * (1.0 / 120.0)
+
+        over_tiles(make_carrier)
+
+        def along_circles(index, inner_carry):
+            field = lax.rem(index * 3, fields)
+
+            @pl.when(jnp.logical_and(turn == 0, field != 1))
+            def _():
+                arrive(field)
+
+            def one(p):
+                value = wrapped(turn, field, p)
+                flux = face_flux(
+                    carrier[p], moved(value, -3), moved(value, -2), moved(value, -1), value,
+                    moved(value, 1), moved(value, 2),
+                )
+                zonal = (flux - moved(flux, 1)) * geo_ref[0]
+                filtered[field, p] = jnp.where(inside, zonal, 0.0)
+
+            over_tiles(one)
+
+            @pl.when(field == 1)
+            def _():
+                def slope(p):
+                    height = wrapped(turn, 0, p) * wrapped(turn, 3, p)
+                    drop = (moved(height, 1) - moved(height, -1)) * (0.5 * gravity_scale)
+                    filtered[field, p] = filtered[field, p] - jnp.where(inside, drop * geo_ref[0], 0.0)
+
+                over_tiles(slope)
+
+            truncate(field)
+            return inner_carry
+
+        lax.fori_loop(0, fields, along_circles, 0)
+
+        def gather_halo(field, inner_carry):
+            take_halo(turn, field)
+            return inner_carry
+
+        lax.fori_loop(0, fields, gather_halo, 0)
+
+        def across_rows(field, inner_carry):
+            def one(p):
+                def at(which, offset):
+                    return states[turn, which, p, 8 + offset : 8 + offset + rows, :]
+
+                below, here, above = at(2, -1), at(2, 0), at(2, 1)
+                around = [at(field, offset) for offset in range(-3, 4)]
+                lower = face_flux((below + here) * (1.0 / 120.0), *around[:6])
+                upper = face_flux((here + above) * (1.0 / 120.0), *around[1:])
+                change = filtered[field, p] + (lower * geo_ref[1] - upper * geo_ref[2])
+                states[turn + 1, field, p, 8 : 8 + rows, :] = around[3] + time_step * change
+
+            over_tiles(one)
+
+            @pl.when(field == 1)
+            def _():
+                def turning(p):
+                    old = states[turn + 1, field, p, 8 : 8 + rows, :]
+                    wind = states[turn, 2, p, 8 : 8 + rows, :]
+                    states[turn + 1, field, p, 8 : 8 + rows, :] = old + time_step * (geo_ref[3] * wind)
+
+                over_tiles(turning)
+
+            @pl.when(field == 2)
+            def _():
+                def turning(p):
+                    old = states[turn + 1, field, p, 8 : 8 + rows, :]
+                    wind = states[turn, 1, p, 8 : 8 + rows, :]
+                    upper = states[turn, 0, p, 9 : 9 + rows, :] * states[turn, 3, p, 9 : 9 + rows, :]
+                    lower = states[turn, 0, p, 7 : 7 + rows, :] * states[turn, 3, p, 7 : 7 + rows, :]
+                    slope = (upper - lower) * (0.5 * gravity_scale)
+                    states[turn + 1, field, p, 8 : 8 + rows, :] = old - time_step * (
+                        geo_ref[3] * wind + slope
+                    )
+
+                over_tiles(turning)
+
+            @pl.when(turn == 0)
+            def _():
+                send_halo(1, field)
+
+            @pl.when(turn == 1)
+            def _():
+                over_peers(lambda peer: last_copy(field, peer, me).start())
+
+            return inner_carry
+
+        lax.fori_loop(0, fields, across_rows, 0)
+        return carry
+
+    lax.fori_loop(0, SUBSTEPS, substep, 0)
+
+    own = pl.multiple_of(band * rows, rows)
+    for field in range(fields):
+        incoming[field, pl.ds(own, rows), :] = states[2, field, me, 8 : 8 + rows, :]
+
+        def arrived(peer, field=field):
+            last_copy(field, peer, peer).wait_recv()
+
+        over_peers(arrived)
+        out_ref[field] = incoming[field].T[:width]
+
+    for field in range(fields):
+
+        def sent(peer, field=field):
+            first_copy(field, peer, me).wait_send()
+            last_copy(field, peer, me).wait_send()
+
+        over_peers(sent)
+
+
+def circle_advance(state, cutoff_row, lon_count, lat_count):
+    fields, _, width, lat_cells = state.shape
+    rows = lat_cells // lon_count
+    lanes = padded_lanes(width)
+    half = lon_count // 2
+    me, lat = lax.axis_index("lon"), lax.axis_index("lat")
+    band = jnp.where(lat % 2 == 0, me, lon_count - 1 - me)
+    centre_cos, centre_sin, face_cos = latitude_rows(
+        lat * lat_cells + band * rows, rows, lat_cells * lat_count
+    )
+    limit = lax.dynamic_slice(cutoff_row, (band * rows,), (rows,))
+    table = jnp.stack([
+        1.0 / centre_cos, face_cos[:-1] / centre_cos, face_cos[1:] / centre_cos,
+        coriolis_scale * centre_sin, limit,
+    ])
+    geometry = jnp.broadcast_to(table[:, :, None], (5, rows, lanes))
+    high, low, twist = circle_tables(lon_count, width, lanes)
+    vmem = pl.BlockSpec(memory_space=pltpu.VMEM)
+    dma = pltpu.SemaphoreType.DMA
+    f32 = jnp.float32
+    result = pl.pallas_call(
+        functools.partial(circle_kernel, lon_count, width, lat_count),
+        out_shape=jax.ShapeDtypeStruct((fields, width, lat_cells), f32),
+        in_specs=[vmem] * 5,
+        out_specs=vmem,
+        scratch_shapes=[
+            pltpu.VMEM((fields, lat_cells, lanes), f32),
+            pltpu.VMEM((3, fields, lon_count, rows + 16, lanes), f32),
+            pltpu.VMEM((fields, lat_cells, lanes), f32),
+            pltpu.VMEM((fields, lon_count, rows, lanes), f32),
+            pltpu.VMEM((lon_count, rows, lanes), f32),
+            pltpu.VMEM((2 * (half + 1) * rows, lanes), f32),
+            pltpu.VMEM((2, 2, fields, 3 * lon_count, lanes), f32),
+            pltpu.VMEM((2, 2, fields, 3 * lon_count, lanes), f32),
+            dma((fields, lon_count)), dma((fields, lon_count)),
+            dma((fields, lon_count)), dma((fields, lon_count)),
+            dma((2, 2, fields)), dma((2, 2, fields)),
+        ],
+        compiler_params=pltpu.CompilerParams(
+            collective_id=0, has_side_effects=True, vmem_limit_bytes=48 * 1024 * 1024
+        ),
+    )(state[:, 0], geometry, twist, high, low)
+    return result[:, None]
+
+
+def padded_lanes(width):
+    return -(-(width + 6) // 128) * 128
+
+
+def fits_circles(state, lon_count, lat_count):
+    fields, levels, width, lat_cells = state.shape
+    return (
+        fields == 5 and levels == 1 and width % 8 == 0 and lat_cells % 128 == 0
+        and lon_count % 4 == 0 and lat_cells == 8 * lon_count and lat_count > 1
+    )
+
+
 def shards(state, cutoffs):
     lat_index = lax.axis_index("lat")
     lat_count = lax.axis_size("lat")
+    lon_count = lax.axis_size("lon")
     lat_cells = state.shape[3]
-    geometry = latitude_rows(lat_index * lat_cells, lat_cells, lat_cells * lat_count)
     is_south = lat_index == 0
     is_north = lat_index == lat_count - 1
+    if fits_circles(state, lon_count, lat_count):
+        unfiltered = lon_count * state.shape[2]
+        north_row = jnp.where(is_north, jnp.flip(cutoffs[1], 0), unfiltered)
+        cutoff_row = jnp.where(is_south, cutoffs[0], north_row).astype(jnp.float32)
+        return circle_advance(state, cutoff_row, lon_count, lat_count)
+    geometry = latitude_rows(lat_index * lat_cells, lat_cells, lat_cells * lat_count)
     north_row = jnp.where(is_north, jnp.flip(cutoffs[1], 0), -1)
     cutoff_row = jnp.where(is_south, cutoffs[0], north_row).astype(jnp.float32)
     for substep_index in range(SUBSTEPS):

time: 314 us -> 99 us (0.32)
  the two profiles are of different devices: /device:TPU:9 before, /device:TPU:0 now
where the time goes in v1:
time: 99 us; the launch traced here: 98.2 us
  Pallas kernels  92.8 us (94%)
  local copies, waits for them, and re-layouts  5.12 us (5%)
    pallas_call x1, Pallas kernels, circle_advance(): pl.pallas_call(functools.partial(circle_kernel, lon_count, width, lat_cou...  92.8 us
    unnamed x11, local copies, waits for them, and re-layouts  4.92 us

profile of v1, /device:TPU:0, one launch (start us, length us, event | category | flops | bytes accessed | tf_op | source)
XLA Modules:
  0.0 98.2 jit_solution(16870130868443881236)
XLA Ops:
  0.0 0.0 copy-start.4
  0.0 0.0 copy-start.3
  0.0 0.7 copy-done.4
  0.7 0.1 rev.4
  0.8 0.1 fusion.5
  0.9 0.1 negate_multiply_fusion
  1.0 0.1 broadcast_in_dim.14.geo_ref
  1.1 0.0 copy-done.3
  1.1 0.0 copy-start
  1.1 1.2 %copy-done = f32[5,1,360,128]{3,2,1,0:T(8,128)S(1)} copy-done((f32[5,1,360,128]{3,2,1,0:T(8,128)S(1)}, f32[5,1,360,128]{3,2,1,0:T(8,128)}, u32[]{:S(2)}) %copy-start) | copy-done | bytes 921624
  2.3 0.0 copy-start.1
  2.3 1.1 %copy-done.1 = bf16[384,768]{1,0:T(8,128)(2,1)S(1)} copy-done((bf16[384,768]{1,0:T(8,128)(2,1)S(1)}, bf16[384,768]{1,0:T(8,128)(2,1)}, u32[]{:S(2)}) %copy-start.1) | copy-done | bytes 589848
  3.3 0.0 copy-start.2
  3.3 1.1 %copy-done.2 = bf16[384,768]{1,0:T(8,128)(2,1)S(1)} copy-done((bf16[384,768]{1,0:T(8,128)(2,1)S(1)}, bf16[384,768]{1,0:T(8,128)(2,1)}, u32[]{:S(2)}) %copy-start.2) | copy-done | bytes 589848
  4.4 92.8 %shard_map.55 = f32[5,360,128]{2,1,0:T(8,128)S(1)} custom-call(f32[5,360,128]{2,1,0:T(8,128)S(1)} %bitcast.15, f32[5,8,384]{2,1,0:T(8,128)S(1)} %broadcast_in_dim.14.geo_ref, f32[2,9,384]{2,1,0:T(8,128)S(1)} %copy-done.3, bf16[384,768]{1,0:T(8,128)(2,1)S(1)} %copy-done.2, bf16[384,768]{1,0:T(8,128)(2,1)S(1)} %copy-done.1), custom_call_target="tpu_custom_call" | custom-call | tf_op jit(solution)/shard_map/pallas_call | solution.py:638
  97.2 0.9 copy.8
  (4 shorter events, 0.1 us)
Async XLA Ops:
  0.0 0.7 copy-start.4
  0.0 1.1 %copy-start.3 = (f32[2,9,384]{2,1,0:T(8,128)S(1)}, f32[2,9,384]{2,1,0:T(8,128)}, u32[]{:S(2)}) copy-start(f32[2,9,384]{2,1,0:T(8,128)} %constant.46.clone.twist_ref) | copy-start | bytes 82948
  1.1 1.2 %copy-start = (f32[5,1,360,128]{3,2,1,0:T(8,128)S(1)}, f32[5,1,360,128]{3,2,1,0:T(8,128)}, u32[]{:S(2)}) copy-start(f32[5,1,360,128]{3,2,1,0:T(8,128)} %param.5) | copy-start | bytes 2764804
  2.3 1.1 %copy-start.1 = (bf16[384,768]{1,0:T(8,128)(2,1)S(1)}, bf16[384,768]{1,0:T(8,128)(2,1)}, u32[]{:S(2)}) copy-start(bf16[384,768]{1,0:T(8,128)(2,1)} %constant.48.clone.low_ref) | copy-start | bytes 1769476
  3.3 1.1 %copy-start.2 = (bf16[384,768]{1,0:T(8,128)(2,1)S(1)}, bf16[384,768]{1,0:T(8,128)(2,1)}, u32[]{:S(2)}) copy-start(bf16[384,768]{1,0:T(8,128)(2,1)} %constant.47.clone.high_ref) | copy-start | bytes 1769476

commit v2 on v1

--- a/solution.py
+++ b/solution.py
@@ -205,8 +205,8 @@
 
 
 def circle_kernel(
-    count, width, bands, x_ref, geo_ref, twist_ref, high_ref, low_ref, out_ref,
-    outgoing, states, incoming, filtered, carrier, spectrum, halo_out, halo_in,
+    count, width, bands, x_hbm, geo_ref, twist_ref, high_hbm, low_hbm, out_ref,
+    x_ref, high_ref, low_ref, x_sem, table_sem, outgoing, states, incoming, filtered, carrier, crossing, spectrum, halo_out, halo_in,
     first_send, first_recv, last_send, last_recv, halo_send, halo_recv,
 ):
     fields = x_ref.shape[0]
@@ -401,9 +401,11 @@
         high = value.astype(jnp.bfloat16)
         low = (value - high.astype(jnp.float32)).astype(jnp.bfloat16)
         weights = high_ref[...]
-        result = jnp.dot(high, weights, preferred_element_type=jnp.float32)
-        result += jnp.dot(low, weights, preferred_element_type=jnp.float32)
-        return result + jnp.dot(high, low_ref[...], preferred_element_type=jnp.float32)
+        both = jnp.dot(
+            jnp.concatenate([high, low], axis=0), weights, preferred_element_type=jnp.float32
+        )
+        rest = jnp.dot(high, low_ref[...], preferred_element_type=jnp.float32)
+        return both[: 2 * block] + both[2 * block :] + rest
 
     def cos_of(k, p):
         return float(np.cos(2.0 * np.pi * (k * p % count) / count))
@@ -479,125 +481,160 @@
                     filtered[field, p, :, cut] = even_part - odd_part
                     filtered[field, count - p, :, cut] = even_part + odd_part
 
-    for index, field in enumerate((1, 0, 3, 4, 2)):
+    def x_copy(field):
+        return pltpu.make_async_copy(x_hbm.at[field], x_ref.at[field], x_sem.at[field])
+
+    table_copies = [
+        pltpu.make_async_copy(high_hbm, high_ref, table_sem.at[0]),
+        pltpu.make_async_copy(low_hbm, low_ref, table_sem.at[1]),
+    ]
+    for field in (1, 2, 0, 3, 4):
+        x_copy(field).start()
+    for copy in table_copies:
+        copy.start()
+
+    def turn_rows(field):
+        x_copy(field).wait()
         source = jnp.concatenate(
             [x_ref[field], jnp.zeros((lanes - width, x_ref.shape[2]), jnp.float32)], axis=0
         )
         outgoing[field] = source.T
-        if index == 0:
-            expected = count - 1 + crosses_south.astype(jnp.int32) + crosses_north.astype(jnp.int32)
-            pl.semaphore_wait(barrier, expected)
-
-        def send(peer, field=field):
-            first_copy(field, peer, me).start()
-
-        over_peers(send)
+
+    def send_circles(field):
+        over_peers(lambda peer: first_copy(field, peer, me).start())
         own = pl.multiple_of(band * rows, rows)
         states[0, field, me, 8 : 8 + rows, :] = outgoing[field, pl.ds(own, rows), :]
 
-    def substep(turn, carry):
-        @pl.when(turn == 0)
-        def _():
-            arrive(1)
-
-        def make_carrier(p):
-            wind = wrapped(turn, 1, p)
-            carrier[p] = (wind + moved(wind, -1)) * (1.0 / 120.0)
-
-        over_tiles(make_carrier)
-
-        def along_circles(index, inner_carry):
-            field = lax.rem(index * 3, fields)
-
-            @pl.when(jnp.logical_and(turn == 0, field != 1))
-            def _():
-                arrive(field)
-
-            def one(p):
-                value = wrapped(turn, field, p)
-                flux = face_flux(
-                    carrier[p], moved(value, -3), moved(value, -2), moved(value, -1), value,
-                    moved(value, 1), moved(value, 2),
-                )
-                zonal = (flux - moved(flux, 1)) * geo_ref[0]
-                filtered[field, p] = jnp.where(inside, zonal, 0.0)
-
-            over_tiles(one)
-
-            @pl.when(field == 1)
-            def _():
-                def slope(p):
-                    height = wrapped(turn, 0, p) * wrapped(turn, 3, p)
-                    drop = (moved(height, 1) - moved(height, -1)) * (0.5 * gravity_scale)
-                    filtered[field, p] = filtered[field, p] - jnp.where(inside, drop * geo_ref[0], 0.0)
-
-                over_tiles(slope)
-
-            truncate(field)
+    turn_rows(1)
+    expected = count - 1 + crosses_south.astype(jnp.int32) + crosses_north.astype(jnp.int32)
+    pl.semaphore_wait(barrier, expected)
+    send_circles(1)
+    for field in (2, 0):
+        turn_rows(field)
+        send_circles(field)
+    for copy in table_copies:
+        copy.wait()
+
+    def advance_field(step_index, carry):
+        turn = step_index // fields
+        index = lax.rem(step_index, fields)
+        field = lax.rem(2 + 3 * index, fields)
+        early = turn == 0
+
+        arrivals = jnp.where(early, jnp.where(index == 0, 2, jnp.where(index == 3, 0, 1)), 0)
+
+        def arrival(order, inner_carry):
+            arrive(jnp.where(index == 0, 1 + order, field))
             return inner_carry
 
-        lax.fori_loop(0, fields, along_circles, 0)
-
-        def gather_halo(field, inner_carry):
-            take_halo(turn, field)
+        lax.fori_loop(0, arrivals, arrival, 0)
+
+        @pl.when(jnp.logical_and(early, index < 2))
+        def _():
+            turn_rows(3 + index)
+            send_circles(3 + index)
+
+        @pl.when(index == 0)
+        def _():
+            def make_carrier(p):
+                wind = wrapped(turn, 1, p)
+                carrier[p] = (wind + moved(wind, -1)) * (geo_ref[0] * (1.0 / 120.0))
+
+            over_tiles(make_carrier, 8)
+
+        def along(p):
+            value = wrapped(turn, field, p)
+            flux = face_flux(
+                carrier[p], moved(value, -3), moved(value, -2), moved(value, -1), value,
+                moved(value, 1), moved(value, 2),
+            )
+            zonal = flux - moved(flux, 1)
+            filtered[field, p] = jnp.where(inside, zonal, 0.0)
+
+        over_tiles(along, 8)
+
+        @pl.when(field == 1)
+        def _():
+            def slope(p):
+                height = wrapped(turn, 0, p) * wrapped(turn, 3, p)
+                drop = (moved(height, 1) - moved(height, -1)) * (0.5 * gravity_scale)
+                filtered[field, p] = filtered[field, p] - jnp.where(inside, drop * geo_ref[0], 0.0)
+
+            over_tiles(slope, 8)
+
+        truncate(field)
+
+        lone = jnp.logical_or(early, jnp.logical_or(field == 1, field == 4))
+        rims = jnp.where(lone, 1, jnp.where(index == 0, 3, 0))
+
+        def gather_halo(order, inner_carry):
+            take_halo(turn, jnp.where(order == 0, field, 3 * (order - 1)))
             return inner_carry
 
-        lax.fori_loop(0, fields, gather_halo, 0)
-
-        def across_rows(field, inner_carry):
-            def one(p):
-                def at(which, offset):
-                    return states[turn, which, p, 8 + offset : 8 + offset + rows, :]
-
-                below, here, above = at(2, -1), at(2, 0), at(2, 1)
-                around = [at(field, offset) for offset in range(-3, 4)]
-                lower = face_flux((below + here) * (1.0 / 120.0), *around[:6])
-                upper = face_flux((here + above) * (1.0 / 120.0), *around[1:])
-                change = filtered[field, p] + (lower * geo_ref[1] - upper * geo_ref[2])
-                states[turn + 1, field, p, 8 : 8 + rows, :] = around[3] + time_step * change
-
-            over_tiles(one)
-
-            @pl.when(field == 1)
-            def _():
-                def turning(p):
-                    old = states[turn + 1, field, p, 8 : 8 + rows, :]
-                    wind = states[turn, 2, p, 8 : 8 + rows, :]
-                    states[turn + 1, field, p, 8 : 8 + rows, :] = old + time_step * (geo_ref[3] * wind)
-
-                over_tiles(turning)
-
-            @pl.when(field == 2)
-            def _():
-                def turning(p):
-                    old = states[turn + 1, field, p, 8 : 8 + rows, :]
-                    wind = states[turn, 1, p, 8 : 8 + rows, :]
-                    upper = states[turn, 0, p, 9 : 9 + rows, :] * states[turn, 3, p, 9 : 9 + rows, :]
-                    lower = states[turn, 0, p, 7 : 7 + rows, :] * states[turn, 3, p, 7 : 7 + rows, :]
-                    slope = (upper - lower) * (0.5 * gravity_scale)
-                    states[turn + 1, field, p, 8 : 8 + rows, :] = old - time_step * (
-                        geo_ref[3] * wind + slope
-                    )
-
-                over_tiles(turning)
-
-            @pl.when(turn == 0)
-            def _():
-                send_halo(1, field)
-
-            @pl.when(turn == 1)
-            def _():
-                over_peers(lambda peer: last_copy(field, peer, me).start())
-
+        lax.fori_loop(0, rims, gather_halo, 0)
+
+        @pl.when(index == 0)
+        def _():
+            def make_crossing(p):
+                below = states[turn, 2, p, 7 : 7 + rows, :]
+                here = states[turn, 2, p, 8 : 8 + rows, :]
+                above = states[turn, 2, p, 9 : 9 + rows, :]
+                crossing[0, p] = (below + here) * (geo_ref[1] * (1.0 / 120.0))
+                crossing[1, p] = (here + above) * (geo_ref[2] * (1.0 / 120.0))
+
+            over_tiles(make_crossing, 8)
+
+        def across(p):
+            around = [
+                states[turn, field, p, 8 + offset : 8 + offset + rows, :] for offset in range(-3, 4)
+            ]
+            lower = face_flux(crossing[0, p], *around[:6])
+            upper = face_flux(crossing[1, p], *around[1:])
+            change = filtered[field, p] + (lower - upper)
+            states[turn + 1, field, p, 8 : 8 + rows, :] = around[3] + time_step * change
+
+        over_tiles(across, 4)
+
+        @pl.when(jnp.logical_or(field == 1, field == 2))
+        def _():
+            sign = jnp.where(field == 1, time_step, -time_step)
+
+            def turning(p):
+                old = states[turn + 1, field, p, 8 : 8 + rows, :]
+                wind = states[turn, 3 - field, p, 8 : 8 + rows, :]
+                states[turn + 1, field, p, 8 : 8 + rows, :] = old + sign * (geo_ref[3] * wind)
+
+            over_tiles(turning, 8)
+
+        @pl.when(jnp.where(early, 1, 2) == field)
+        def _():
+            def climb(p):
+                old = states[turn + 1, 2, p, 8 : 8 + rows, :]
+                upper = states[turn, 0, p, 9 : 9 + rows, :] * states[turn, 3, p, 9 : 9 + rows, :]
+                lower = states[turn, 0, p, 7 : 7 + rows, :] * states[turn, 3, p, 7 : 7 + rows, :]
+                slope = (upper - lower) * (0.5 * gravity_scale * time_step)
+                states[turn + 1, 2, p, 8 : 8 + rows, :] = old - slope
+
+            over_tiles(climb, 8)
+
+        leaving = jnp.where(early, jnp.where(field == 2, 0, jnp.where(field == 1, 2, 1)), 0)
+
+        def spread_halo(order, inner_carry):
+            send_halo(1, jnp.where(order == 0, field, 2))
             return inner_carry
 
-        lax.fori_loop(0, fields, across_rows, 0)
+        lax.fori_loop(0, leaving, spread_halo, 0)
+
+        @pl.when(turn == 1)
+        def _():
+            over_peers(lambda peer: last_copy(field, peer, me).start())
+
         return carry
 
-    lax.fori_loop(0, SUBSTEPS, substep, 0)
+    lax.fori_loop(0, SUBSTEPS * fields, advance_field, 0)
 
     own = pl.multiple_of(band * rows, rows)
-    for field in range(fields):
+    for field in (2, 0, 3, 1, 4):
         incoming[field, pl.ds(own, rows), :] = states[2, field, me, 8 : 8 + rows, :]
 
         def arrived(peer, field=field):
@@ -633,19 +670,25 @@
     geometry = jnp.broadcast_to(table[:, :, None], (5, rows, lanes))
     high, low, twist = circle_tables(lon_count, width, lanes)
     vmem = pl.BlockSpec(memory_space=pltpu.VMEM)
+    hbm = pl.BlockSpec(memory_space=pltpu.HBM)
     dma = pltpu.SemaphoreType.DMA
     f32 = jnp.float32
     result = pl.pallas_call(
         functools.partial(circle_kernel, lon_count, width, lat_count),
         out_shape=jax.ShapeDtypeStruct((fields, width, lat_cells), f32),
-        in_specs=[vmem] * 5,
+        in_specs=[hbm, vmem, vmem, hbm, hbm],
         out_specs=vmem,
         scratch_shapes=[
+            pltpu.VMEM((fields, width, lat_cells), f32),
+            pltpu.VMEM(high.shape, high.dtype),
+            pltpu.VMEM(low.shape, low.dtype),
+            dma((fields,)), dma((2,)),
             pltpu.VMEM((fields, lat_cells, lanes), f32),
             pltpu.VMEM((3, fields, lon_count, rows + 16, lanes), f32),
             pltpu.VMEM((fields, lat_cells, lanes), f32),
             pltpu.VMEM((fields, lon_count, rows, lanes), f32),
             pltpu.VMEM((lon_count, rows, lanes), f32),
+            pltpu.VMEM((2, lon_count, rows, lanes), f32),
             pltpu.VMEM((2 * (half + 1) * rows, lanes), f32),
             pltpu.VMEM((2, 2, fields, 3 * lon_count, lanes), f32),
             pltpu.VMEM((2, 2, fields, 3 * lon_count, lanes), f32),
@@ -654,7 +697,7 @@
             dma((2, 2, fields)), dma((2, 2, fields)),
         ],
         compiler_params=pltpu.CompilerParams(
-            collective_id=0, has_side_effects=True, vmem_limit_bytes=48 * 1024 * 1024
+            collective_id=0, has_side_effects=True, vmem_limit_bytes=62 * 1024 * 1024
         ),
     )(state[:, 0], geometry, twist, high, low)
     return result[:, None]

time: 99 us -> 80.4 us (0.81)
  Pallas kernels: 92.8 us -> 76.3 us
  local copies, waits for them, and re-layouts: 5.12 us -> 3.68 us
    pallas_call x1, Pallas kernels: 92.8 us -> 76.3 us  [circle_advance(): pl.pallas_call(functools.partial(circle_kernel, lon_count, width, lat_cou...]
    unnamed x11 -> x3, local copies, waits for them, and re-layouts: 4.92 us -> 2.84 us
where the time goes in v2:
time: 80.4 us; the launch traced here: 80.2 us
  Pallas kernels  76.3 us (95%)
  local copies, waits for them, and re-layouts  3.68 us (5%)
    pallas_call x1, Pallas kernels, circle_advance(): pl.pallas_call(functools.partial(circle_kernel, lon_count, width, lat_cou...  76.3 us
    unnamed x3, local copies, waits for them, and re-layouts  2.84 us

profile of v2, /device:TPU:0, one launch (start us, length us, event | category | flops | bytes accessed | tf_op | source)
XLA Modules:
  0.0 80.2 jit_solution(10218434048027095217)
XLA Ops:
  0.0 0.0 copy-start
  0.0 0.7 copy-done
  0.7 0.1 rev.4
  0.8 0.1 fusion.5
  0.9 0.1 negate_multiply_fusion
  1.0 0.7 broadcast_in_dim.14.geo_ref
  1.7 76.3 %shard_map.55 = f32[5,360,128]{2,1,0:T(8,128)} custom-call(f32[5,360,128]{2,1,0:T(8,128)} %bitcast.15, f32[5,8,384]{2,1,0:T(8,128)} %broadcast_in_dim.14.geo_ref, f32[2,9,384]{2,1,0:T(8,128)} %constant.46.clone.twist_ref, bf16[384,768]{1,0:T(8,128)(2,1)} %constant.47.clone.high_hbm, bf16[384,768]{1,0:T(8,128)(2,1)} %constant.48.clone.low_hbm), custom_call_target="tpu_custom_call" | custom-call | tf_op jit(solution)/shard_map/pallas_call | solution.py:676
  78.0 2.2 %copy.8 = f32[5,1,360,128]{3,2,1,0:T(8,128)} copy(f32[5,1,360,128]{3,2,1,0:T(8,128)} %bitcast.14) | data formatting | bytes 1843200
  (4 shorter events, 0.1 us)
Async XLA Ops:
  0.0 0.7 copy-start

commit v3 on v2

--- a/solution.py
+++ b/solution.py
@@ -509,7 +509,7 @@
     expected = count - 1 + crosses_south.astype(jnp.int32) + crosses_north.astype(jnp.int32)
     pl.semaphore_wait(barrier, expected)
     send_circles(1)
-    for field in (2, 0):
+    for field in (2,):
         turn_rows(field)
         send_circles(field)
     for copy in table_copies:
@@ -524,12 +524,20 @@
         arrivals = jnp.where(early, jnp.where(index == 0, 2, jnp.where(index == 3, 0, 1)), 0)
 
         def arrival(order, inner_carry):
-            arrive(jnp.where(index == 0, 1 + order, field))
+            coming = jnp.where(index == 0, 1 + order, field)
+            arrive(coming)
+
+            @pl.when(coming < 3)
+            def _():
+                ahead = jnp.where(coming == 1, 0, jnp.where(coming == 2, 3, 4))
+                turn_rows(ahead)
+                send_circles(ahead)
+
             return inner_carry
 
         lax.fori_loop(0, arrivals, arrival, 0)
 
-        @pl.when(jnp.logical_and(early, index < 2))
+        @pl.when(step_index < 0)
         def _():
             turn_rows(3 + index)
             send_circles(3 + index)
@@ -673,6 +681,7 @@
     hbm = pl.BlockSpec(memory_space=pltpu.HBM)
     dma = pltpu.SemaphoreType.DMA
     f32 = jnp.float32
+    keep = lambda value: pltpu.with_memory_space_constraint(value, pltpu.HBM)
     result = pl.pallas_call(
         functools.partial(circle_kernel, lon_count, width, lat_count),
         out_shape=jax.ShapeDtypeStruct((fields, width, lat_cells), f32),
@@ -697,9 +706,9 @@
             dma((2, 2, fields)), dma((2, 2, fields)),
         ],
         compiler_params=pltpu.CompilerParams(
-            collective_id=0, has_side_effects=True, vmem_limit_bytes=62 * 1024 * 1024
+            collective_id=0, has_side_effects=True, vmem_limit_bytes=48 * 1024 * 1024
         ),
-    )(state[:, 0], geometry, twist, high, low)
+    )(keep(state[:, 0]), geometry, twist, keep(jnp.asarray(high)), keep(jnp.asarray(low)))
     return result[:, None]
 
 

time: 80.4 us -> 76.2 us (0.948)
  Pallas kernels: 76.3 us -> 74 us
  local copies, waits for them, and re-layouts: 3.68 us -> 1.8 us
    pallas_call x1, Pallas kernels: 76.3 us -> 74 us  [circle_advance(): pl.pallas_call(functools.partial(circle_kernel, lon_count, width, lat_cou...]
    unnamed x3 -> x5, local copies, waits for them, and re-layouts: 2.84 us -> 1.61 us
where the time goes in v3:
time: 76.2 us; the launch traced here: 76 us
  Pallas kernels  74 us (97%)
  local copies, waits for them, and re-layouts  1.8 us (2%)
    pallas_call x1, Pallas kernels, circle_advance(): pl.pallas_call(functools.partial(circle_kernel, lon_count, width, lat_cou...  74 us
    unnamed x5, local copies, waits for them, and re-layouts  1.61 us

profile of v3, /device:TPU:0, one launch (start us, length us, event | category | flops | bytes accessed | tf_op | source)
XLA Modules:
  0.0 76.0 jit_solution(16590925431147213871)
XLA Ops:
  0.0 0.0 copy-start.1
  0.0 0.0 copy-start
  0.0 0.7 copy-done.1
  0.7 0.1 rev.4
  0.8 0.1 fusion.5
  0.9 0.1 negate_multiply_fusion
  1.0 0.1 broadcast_in_dim.14.geo_ref
  1.1 0.0 copy-done
  1.1 74.0 %shard_map.55 = f32[5,360,128]{2,1,0:T(8,128)S(1)} custom-call(f32[5,360,128]{2,1,0:T(8,128)} %bitcast.15, f32[5,8,384]{2,1,0:T(8,128)S(1)} %broadcast_in_dim.14.geo_ref, f32[2,9,384]{2,1,0:T(8,128)S(1)} %copy-done, bf16[384,768]{1,0:T(8,128)(2,1)} %constant.46.clone.high_hbm, bf16[384,768]{1,0:T(8,128)(2,1)} %constant.47.clone.low_hbm), custom_call_target="tpu_custom_call" | custom-call | tf_op jit(solution)/shard_map/pallas_call | solution.py:685
  75.1 0.9 %copy.8 = f32[5,1,360,128]{3,2,1,0:T(8,128)} copy(f32[5,1,360,128]{3,2,1,0:T(8,128)S(1)} %bitcast.14) | data formatting | bytes 1843200
  (4 shorter events, 0.1 us)
Async XLA Ops:
  0.0 0.7 copy-start.1
  0.0 1.1 %copy-start = (f32[2,9,384]{2,1,0:T(8,128)S(1)}, f32[2,9,384]{2,1,0:T(8,128)}, u32[]{:S(2)}) copy-start(f32[2,9,384]{2,1,0:T(8,128)} %constant.48.clone.twist_ref) | copy-start | bytes 82948
